TPU v7x, 32 devices: a whole 2x2x4 slice. The times are simulated.
32 devices in a mesh: ctx: 8 (over y, x, core), tp: 4 (over z).
Axes of the slice: x: 2, y: 2, z: 4, core: 2. Of those that a mesh axis runs over, the one named last changes fastest.
Arguments:
- queries: bfloat16 [1024, 32, 128], P('ctx', 'tp'), may hold values from -8 to 8
- window_keys: bfloat16 [1024, 4, 128], P('ctx', 'tp'), may hold values from -8 to 8
- window_values: bfloat16 [1024, 4, 128], P('ctx', 'tp'), may hold values from -6 to 6
- anchor_keys: bfloat16 [512, 4, 128], P('ctx', 'tp'), may hold values from -8 to 8
- anchor_values: bfloat16 [512, 4, 128], P('ctx', 'tp'), may hold values from -6 to 6
- passing_rows: int32 [8, 32], replicated, may hold values from 0 to 127, as said below
- block_of_device: int32 [8], replicated, may hold values from 0 to 7, each once
- out_weight: bfloat16 [4096, 4096], P(None, 'tp'), may hold values from -0.09375 to 0.09375
Outputs:
- mixed: bfloat16 [4096, 1024], P('tp', 'ctx')
Inputs may be any that keep to these rules, and one draw needn't show every extreme that they name: `passing_rows`: each row holds 32 different positions. `block_of_device`: every block number appears once.
All inputs are finite; a program needn't handle non-finite values.
Results may differ from a plain program's by a relative error of at most 0.013.
Values may be sent and summed in bfloat16 or wider, within the bound.
No kernel may reach another device: no remote copies, remote signals or barrier semaphores. Data moves between devices by JAX's collectives and lax.ppermute only.
A program may use at most 128 MiB of HBM per device.

v0:
```python
import jax
import jax.numpy as jnp
from jax import lax
from jax.sharding import PartitionSpec as P


def lookup(lookup_table, slot_ids):
    matches = slot_ids[:, None] == jnp.arange(lookup_table.shape[0], dtype=jnp.int32)[None, :]
    return jnp.sum(jnp.where(matches, lookup_table[None, :], 0), axis=1)


def attend(fold_state, grouped, key_rows, value_rows, visible):
    running_max, running_sum, weighted = fold_state
    key_count = key_rows.shape[0]
    score_scale = grouped.shape[-1] ** (-0.5)
    for first_key in range(0, key_count, 1024):
        last_key = min(first_key + 1024, key_count)
        visible_part = visible[:, first_key:last_key][:, None, None, :]
        scores = (
            jnp.einsum(
                "tgjd,ngd->tgjn",
                grouped,
                key_rows[first_key:last_key],
                preferred_element_type=jnp.float32,
            )
            * score_scale
        )
        scores = jnp.where(visible_part, scores, -1e30)
        new_max = jnp.maximum(running_max, jnp.max(scores, axis=-1))
        weights = jnp.where(visible_part, jnp.exp(scores - new_max[..., None]), 0.0)
        factor = jnp.exp(running_max - new_max)
        running_sum = running_sum * factor + jnp.sum(weights, axis=-1)
        weighted = weighted * factor[..., None] + jnp.einsum(
            "tgjn,ngd->tgjd",
            weights.astype(jnp.bfloat16),
            value_rows[first_key:last_key],
            preferred_element_type=jnp.float32,
        )
        running_max = new_max
    return (running_max, running_sum, weighted)


def body(
    queries,
    window_keys,
    window_values,
    anchor_keys,
    anchor_values,
    passing_rows,
    block_of_device,
    out_weight,
):
    tok_rows, head_count, head_size = queries.shape
    kv_local = window_keys.shape[1]
    group_size = head_count // kv_local
    retained = passing_rows.shape[1]
    grouped = queries.reshape(tok_rows, kv_local, group_size, head_size)
    my_slot = lax.axis_index("ctx")
    own_block = lookup(block_of_device, jnp.reshape(my_slot, (1,)))[0]
    fold_state = (
        jnp.full((tok_rows, kv_local, group_size), -1e30, jnp.float32),
        jnp.zeros((tok_rows, kv_local, group_size), jnp.float32),
        jnp.zeros((tok_rows, kv_local, group_size, head_size), jnp.float32),
    )
    places = jnp.arange(tok_rows, dtype=jnp.int32)
    causal = places[None, :] <= places[:, None]
    fold_state = attend(fold_state, grouped, window_keys, window_values, causal)
    shard_piece = (
        lax.all_gather(anchor_keys, "ctx", axis=0, tiled=True),
        lax.all_gather(anchor_values, "ctx", axis=0, tiled=True),
    )
    seen_all = jnp.ones((1, shard_piece[0].shape[0]), dtype=bool)
    fold_state = attend(fold_state, grouped, shard_piece[0], shard_piece[1], seen_all)
    chosen = lax.dynamic_slice_in_dim(passing_rows, my_slot, 1, 0)[0]
    picked_keys = jnp.take(window_keys, chosen, axis=0)
    picked_values = jnp.take(window_values, chosen, axis=0)
    shard_piece = (
        lax.all_gather(picked_keys, "ctx", axis=0, tiled=True),
        lax.all_gather(picked_values, "ctx", axis=0, tiled=True),
    )
    rows_here = shard_piece[0].shape[0]
    slot_ids = jnp.arange(rows_here, dtype=jnp.int32) // retained
    earlier = lookup(block_of_device, slot_ids) < own_block
    fold_state = attend(fold_state, grouped, shard_piece[0], shard_piece[1], earlier[None, :])
    running_max, running_sum, weighted = fold_state
    attended = (
        (weighted / running_sum[..., None])
        .reshape(tok_rows, head_count * head_size)
        .astype(jnp.bfloat16)
    )
    return lax.psum_scatter(
        lax.dot_general(
            out_weight, attended, (((1,), (1,)), ((), ())), preferred_element_type=jnp.float32
        ).astype(jnp.bfloat16),
        "tp",
        scatter_dimension=0,
        tiled=True,
    )


def solution(mesh):
    placed = (
        P("ctx", "tp", None),
        P("ctx", "tp", None),
        P("ctx", "tp", None),
        P("ctx", "tp", None),
        P("ctx", "tp", None),
        P(),
        P(),
        P(None, "tp"),
    )
    return jax.shard_map(
        body, mesh=mesh, in_specs=placed, out_specs=P("tp", "ctx"), check_vma=False
    )
```

profile of v0, /device:TPU:0, one launch (start us, length us, event | category | flops | bytes accessed | tf_op | source)
XLA Modules:
  0.0 95.2 jit_solution(17954474765099559327)
XLA Ops:
  6.5 0.0 copy-start
  6.5 0.0 reduce-scatter.2.cloned.1.call-start
  6.6 0.7 compare_and_fusion
  7.3 1.3 %gather_fusion = bf16[32,128]{1,0:T(8,128)(2,1)S(1)} fusion(bf16[128,128]{1,0:T(8,128)(2,1)} %bitcast.112, s32[1024]{0:T(1024)S(1)} %pad_clamp_fusion), kind=kCustom, calls=%fused_computation.clone | custom fusion | bytes 16512 | tf_op jit(solution)/shard_map/jit(_take)/gather | solution.py:75
  8.7 1.3 %gather_fusion.1 = bf16[32,128]{1,0:T(8,128)(2,1)S(1)} fusion(bf16[128,128]{1,0:T(8,128)(2,1)} %bitcast.114, s32[1024]{0:T(1024)S(1)} %pad_clamp_fusion), kind=kCustom, calls=%fused_computation.1.clone | custom fusion | bytes 16512 | tf_op jit(solution)/shard_map/jit(_take)/gather | solution.py:76
  10.0 0.1 bitcast_select_fusion
  10.1 10.7 %all_gather.14 = bf16[256,1,128]{2,0,1:T(8,128)(2,1)S(1)} all-gather(bf16[32,1,128]{2,0,1:T(8,128)(2,1)S(1)} %get-tuple-element.16), channel_id=1, replica_groups=mesh['ctx'=8,'tp'=4] {'ctx'}, dimensions={0}, use_global_device_ids=true | all-gather | bytes 73728 | tf_op jit(solution)/shard_map/all_gather | solution.py:78
  20.8 1.3 %fusion.44 = s32[]{:T(128)} fusion(s32[8]{0:T(128)} %param.16, s32[]{:T(128)S(6)} %axis_index.15), kind=kLoop, calls=%fused_computation.71 | loop fusion | flops 23 | bytes 40 | tf_op jit(solution)/shard_map/reduce_sum | solution.py:9
  22.1 0.7 select_reduce_fusion
  22.8 9.2 %all_gather.12 = bf16[512,1,128]{2,0,1:T(8,128)(2,1)S(1)} all-gather(bf16[64,1,128]{2,0,1:T(8,128)(2,1)} %param.13), channel_id=1, replica_groups=mesh['ctx'=8,'tp'=4] {'ctx'}, dimensions={0}, use_global_device_ids=true | all-gather | bytes 147456 | tf_op jit(solution)/shard_map/all_gather | solution.py:69
  32.0 0.0 copy-done
  32.0 1.0 %fusion.52 = (f32[128,8]{0,1:T(8,128)S(1)}, f32[128,1,8,128]{0,3,2,1:T(8,128)S(1)}) fusion(bf16[128,8,128]{2,1,0:T(8,128)(2,1)S(1)} %copy-done, bf16[128,1,128]{2,0,1:T(8,128)(2,1)} %param.11, pred[128,128]{0,1:T(8,128)(4,1)S(1)} %iota_compare_fusion), kind=kOutput, calls=%fused_computation.79 | convolution fusion | flops 33946624 | bytes 839680 | tf_op jit(solution)/shard_map/tgjd,ngd->tgjn/dot_general | solution.py:20
  33.0 0.0 slice-start
  33.0 0.4 bitcast_reduce_fusion
  33.5 0.0 copy-start.2
  33.5 8.7 %all_gather.15 = bf16[256,1,128]{2,0,1:T(8,128)(2,1)S(1)} all-gather(bf16[32,1,128]{2,0,1:T(8,128)(2,1)S(1)} %get-tuple-element.15), channel_id=1, replica_groups=mesh['ctx'=8,'tp'=4] {'ctx'}, dimensions={0}, use_global_device_ids=true | all-gather | bytes 73728 | tf_op jit(solution)/shard_map/all_gather | solution.py:79
  42.2 0.6 broadcast_compare_fusion
  42.9 0.3 fusion.51
  43.2 0.2 fusion.20
  43.4 0.3 convolution_bitcast_fusion.1
  43.8 0.0 copy-done.2
  43.8 9.0 %all_gather.13 = bf16[512,1,128]{2,0,1:T(8,128)(2,1)S(1)} all-gather(bf16[64,1,128]{2,0,1:T(8,128)(2,1)S(1)} %copy-done.2), channel_id=1, replica_groups=mesh['ctx'=8,'tp'=4] {'ctx'}, dimensions={0}, use_global_device_ids=true | all-gather | bytes 147456 | tf_op jit(solution)/shard_map/all_gather | solution.py:70
  52.8 0.0 slice-start.1
  52.8 0.4 fusion.2
  53.1 0.0 copy-start.1
  53.1 0.5 convolution_bitcast_fusion
  53.7 0.1 fusion.27
  53.8 0.3 copy-done.1
  54.1 0.3 fusion.14
  54.4 0.0 slice-done
  54.4 0.5 slice-done.1
  55.0 3.8 %fusion = bf16[4096,128]{0,1:T(8,128)(2,1)} fusion(bf16[128,1024]{0,1:T(8,128)(2,1)S(1)} %bitcast.113, bf16[4096,1024]{1,0:T(8,128)(2,1)S(1)} %bitcast.111), kind=kOutput, calls=%fused_computation.3 | convolution fusion | flops 1074266112 | bytes 9699328 | tf_op jit(solution)/shard_map/dot_general | solution.py:92
  58.8 0.0 reduce-scatter.2.cloned.1.call-update
  58.9 27.7 %reduce-scatter.2.cloned.1.call-done = bf16[1024,128]{0,1:T(8,128)(2,1)} async-done(((bf16[4096,128]{0,1:T(8,128)(2,1)}), bf16[1024,128]{0,1:T(8,128)(2,1)}) %reduce-scatter.2.cloned.1.call-update) | async-done | bytes 262160 | tf_op jit(solution)/shard_map/reduce_scatter | solution.py:91
  86.6 1.8 %copy.38 = bf16[1024,128]{1,0:T(8,128)(2,1)} copy(bf16[1024,128]{0,1:T(8,128)(2,1)} %reduce-scatter.2.cloned.1.call-done) | data formatting | bytes 524288 | tf_op jit(solution)/shard_map/reduce_scatter | solution.py:91
  (6 shorter events, 0.1 us)
Async XLA Ops:
  6.5 25.5 %copy-start = (bf16[128,8,128]{2,1,0:T(8,128)(2,1)S(1)}, bf16[128,8,128]{2,1,0:T(8,128)(2,1)}, u32[]{:S(2)}) copy-start(bf16[128,8,128]{2,1,0:T(8,128)(2,1)} %param.10) | copy-start | bytes 786436
  6.5 80.0 %reduce-scatter.2.cloned.1.call-start = ((), (), s32[]{:S(2)}) async-start(), calls=%async_computation.1 | async-start | bytes 1310720 | tf_op jit(solution)/shard_map/reduce_scatter | solution.py:91
  33.0 21.4 %slice-start = ((s8[8388608]{0:T(1024)(128)(4,1)}), s8[4194304]{0:T(1024)(128)(4,1)S(1)}, s32[]{:S(2)}) async-start(s8[8388608]{0:T(1024)(128)(4,1)} %bitcast.110), calls=%async_computation.2 | async-start | bytes 8388608
  33.5 10.3 %copy-start.2 = (bf16[64,1,128]{2,0,1:T(8,128)(2,1)S(1)}, bf16[64,1,128]{2,0,1:T(8,128)(2,1)}, u32[]{:S(2)}) copy-start(bf16[64,1,128]{2,0,1:T(8,128)(2,1)} %param.14) | copy-start | bytes 49156
  52.8 2.2 %slice-start.1 = ((s8[8388608]{0:T(1024)(128)(4,1)}), s8[4194304]{0:T(1024)(128)(4,1)S(1)}, s32[]{:S(2)}) async-start(s8[8388608]{0:T(1024)(128)(4,1)} %bitcast.110), calls=%async_computation.3 | async-start | bytes 8388608
  53.1 0.9 copy-start.1
Sparse Core Ops, SparseCore 0:
  59.0 27.5 reduce-scatter.1
where the time goes:
time: 95.7 us; the launch traced here: 95.2 us
  blocking collectives  37.6 us (39%)
  waiting for transfers between devices  27.7 us (29%)
  between operations  13.5 us (14%)
  matrix products  6.79 us (7%)
  local copies, waits for them, and re-layouts  5.3 us (6%)
  other arithmetic  4.22 us (4%)
    reduce_scatter x1, waiting for transfers between devices, body(): lax.psum_scatter(lax.dot_general(out_weight, attended, (((1,), (1,)), (()...  27.7 us
    all_gather x1, blocking collectives, body(): lax.all_gather(picked_keys, 'ctx', axis=0, tiled=True)  10.7 us
    all_gather x1, blocking collectives, body(): lax.all_gather(anchor_keys, 'ctx', axis=0, tiled=True)  9.17 us
    all_gather x1, blocking collectives, body(): lax.all_gather(anchor_values, 'ctx', axis=0, tiled=True)  9.01 us
    all_gather x1, blocking collectives, body(): lax.all_gather(picked_values, 'ctx', axis=0, tiled=True)  8.72 us
    dot_general x1, matrix products, body(): lax.dot_general(out_weight, attended, (((1,), (1,)), ((), ())), preferred...  3.84 us
    reduce_sum x2, other arithmetic, lookup(): return jnp.sum(jnp.where(matches, lookup_table[None, :], 0), axis=1)  2.03 us
  transfers between devices with their start and end apart: 1, of which 1 were waited for; matrix products, arithmetic and copies ran while one was open for 0% of the time, Pallas kernels for 0%

commit v1 on v0

--- a/solution.py
+++ b/solution.py
@@ -2,6 +2,22 @@
 import jax.numpy as jnp
 from jax import lax
 from jax.sharding import PartitionSpec as P
+
+
+def gather_around(x, axis, dim):
+    ways, here, step = (lax.axis_size(axis), lax.axis_index(axis), x.shape[dim])
+    dims = [n * ways if d == dim else n for d, n in enumerate(x.shape)]
+    full = lax.dynamic_update_slice_in_dim(jnp.zeros(dims, x.dtype), x, here * step, axis=dim)
+    going_up = going_down = x
+    for far in range(1, ways // 2 + 1):
+        going_up = lax.ppermute(going_up, axis, [(d, (d + 1) % ways) for d in range(ways)])
+        full = lax.dynamic_update_slice_in_dim(full, going_up, (here - far) % ways * step, axis=dim)
+        if 2 * far < ways:
+            going_down = lax.ppermute(going_down, axis, [(d, (d - 1) % ways) for d in range(ways)])
+            full = lax.dynamic_update_slice_in_dim(
+                full, going_down, (here + far) % ways * step, axis=dim
+            )
+    return full
 
 
 def lookup(lookup_table, slot_ids):
@@ -67,7 +83,7 @@
     fold_state = attend(fold_state, grouped, window_keys, window_values, causal)
     shard_piece = (
         lax.all_gather(anchor_keys, "ctx", axis=0, tiled=True),
-        lax.all_gather(anchor_values, "ctx", axis=0, tiled=True),
+        gather_around(anchor_values, "ctx", 0),
     )
     seen_all = jnp.ones((1, shard_piece[0].shape[0]), dtype=bool)
     fold_state = attend(fold_state, grouped, shard_piece[0], shard_piece[1], seen_all)

time: 95.7 us -> 118 us (1.23)
  local copies, waits for them, and re-layouts: 5.3 us -> 23.3 us
  blocking collectives: 37.6 us -> 27.7 us
  starting transfers between devices: 0.01 us -> 7.58 us
  matrix products: 6.79 us -> 10.2 us
  waiting for transfers between devices: 27.7 us -> 30.3 us
    another operation x0 -> x9, local copies, waits for them, and re-layouts: none -> 10.7 us
    all_gather x1 -> x0, blocking collectives: 9.01 us -> none  [body(): lax.all_gather(anchor_values, 'ctx', axis=0, tiled=True)]
    dynamic_update_slice x0 -> x8, local copies, waits for them, and re-layouts: none -> 8.07 us  [the longest x4 3.97 us: gather_around(): lax.dynamic_update_slice_in_dim(full, going_up, (here - far) % ways * ste...]
    ppermute x0 -> x7, starting transfers between devices: none -> 7.58 us  [the longest x3 6.68 us: gather_around(): lax.ppermute(going_down, axis, [(d, (d - 1) % ways) for d in range(ways)])]
    dot_general x1, matrix products: 3.84 us -> 7.27 us  [body(): lax.dot_general(out_weight, attended, (((1,), (1,)), ((), ())), preferred...]
    ppermute x0 -> x7, waiting for transfers between devices: none -> 1.35 us  [the longest x4 1.34 us: gather_around(): lax.ppermute(going_up, axis, [(d, (d + 1) % ways) for d in range(ways)])]
    reduce_scatter x1, waiting for transfers between devices: 27.7 us -> 28.9 us  [body(): lax.psum_scatter(lax.dot_general(out_weight, attended, (((1,), (1,)), (()...]
  transfers between devices with their start and end apart: 1 -> 8, of which waited for: 1 -> 2; matrix products, arithmetic and copies ran while one was open for 0% -> 22% of each run, Pallas kernels for 0% -> 0%
where the time goes in v1:
time: 118 us; the launch traced here: 117 us
  waiting for transfers between devices  30.3 us (26%)
  blocking collectives  27.7 us (23%)
  local copies, waits for them, and re-layouts  23.3 us (20%)
  between operations  13.8 us (12%)
  matrix products  10.2 us (9%)
  starting transfers between devices  7.58 us (6%)
  other arithmetic  4.19 us (4%)
    reduce_scatter x1, waiting for transfers between devices, body(): lax.psum_scatter(lax.dot_general(out_weight, attended, (((1,), (1,)), (()...  28.9 us
    another operation x9, local copies, waits for them, and re-layouts  10.7 us
    all_gather x1, blocking collectives, body(): lax.all_gather(picked_keys, 'ctx', axis=0, tiled=True)  10 us
    all_gather x1, blocking collectives, body(): lax.all_gather(picked_values, 'ctx', axis=0, tiled=True)  9.29 us
    all_gather x1, blocking collectives, body(): lax.all_gather(anchor_keys, 'ctx', axis=0, tiled=True)  8.39 us
    dot_general x1, matrix products, body(): lax.dot_general(out_weight, attended, (((1,), (1,)), ((), ())), preferred...  7.27 us
    ppermute x3, starting transfers between devices, gather_around(): lax.ppermute(going_down, axis, [(d, (d - 1) % ways) for d in range(ways)])  6.68 us
    dynamic_update_slice x4, local copies, waits for them, and re-layouts, gather_around(): lax.dynamic_update_slice_in_dim(full, going_up, (here - far) % ways * ste...  3.97 us
  transfers between devices with their start and end apart: 8, of which 2 were waited for; matrix products, arithmetic and copies ran while one was open for 22% of the time, Pallas kernels for 0%

profile of v1, /device:TPU:0, one launch (start us, length us, event | category | flops | bytes accessed | tf_op | source)
XLA Modules:
  0.0 117.0 jit_solution(3229611965945485571)
XLA Ops:
  6.5 0.5 collective-permute-start
  7.0 2.9 %collective-permute-start.1 = (bf16[64,1,128]{2,0,1:T(8,128)(2,1)}, bf16[64,1,128]{2,0,1:T(8,128)(2,1)S(1)}, u32[]{:S(2)}, u32[]{:S(2)}) collective-permute-start(bf16[64,1,128]{2,0,1:T(8,128)(2,1)} %param.14), channel_id=1, source_target_pairs={{0,28},{4,0},{8,4},{12,8},{16,12},{20,16},{24,20},{28,24},{1,29},{... | collective-permute-start | bytes 49160 | tf_op jit(solution)/shard_map/ppermute | solution.py:16
  9.9 0.7 compare_and_fusion
  10.6 1.3 %gather_fusion = bf16[32,128]{1,0:T(8,128)(2,1)S(1)} fusion(bf16[128,128]{1,0:T(8,128)(2,1)} %bitcast.114, s32[1024]{0:T(1024)S(1)} %pad_clamp_fusion), kind=kCustom, calls=%fused_computation.clone | custom fusion | bytes 16512 | tf_op jit(solution)/shard_map/jit(_take)/gather | solution.py:91
  12.0 1.3 %gather_fusion.1 = bf16[32,128]{1,0:T(8,128)(2,1)S(1)} fusion(bf16[128,128]{1,0:T(8,128)(2,1)} %bitcast.115, s32[1024]{0:T(1024)S(1)} %pad_clamp_fusion), kind=kCustom, calls=%fused_computation.1.clone | custom fusion | bytes 16512 | tf_op jit(solution)/shard_map/jit(_take)/gather | solution.py:92
  13.3 0.1 bitcast_select_fusion
  13.4 10.0 %all_gather.10 = bf16[256,1,128]{2,0,1:T(8,128)(2,1)S(1)} all-gather(bf16[32,1,128]{2,0,1:T(8,128)(2,1)S(1)} %get-tuple-element.16), channel_id=1, replica_groups=mesh['ctx'=8,'tp'=4] {'ctx'}, dimensions={0}, use_global_device_ids=true | all-gather | bytes 73728 | tf_op jit(solution)/shard_map/all_gather | solution.py:94
  23.4 1.3 %fusion.44 = s32[]{:T(128)} fusion(s32[8]{0:T(128)} %param.16, s32[]{:T(128)S(6)} %axis_index.19), kind=kLoop, calls=%fused_computation.71 | loop fusion | flops 23 | bytes 40 | tf_op jit(solution)/shard_map/reduce_sum | solution.py:25
  24.7 0.7 select_reduce_fusion
  25.4 8.4 %all_gather.9 = bf16[512,1,128]{2,0,1:T(8,128)(2,1)S(1)} all-gather(bf16[64,1,128]{2,0,1:T(8,128)(2,1)} %param.13), channel_id=1, replica_groups=mesh['ctx'=8,'tp'=4] {'ctx'}, dimensions={0}, use_global_device_ids=true | all-gather | bytes 147456 | tf_op jit(solution)/shard_map/all_gather | solution.py:85
  33.8 1.0 fusion.52
  34.8 0.4 bitcast_reduce_fusion
  35.3 0.7 broadcast_compare_fusion
  35.9 0.3 fusion.51
  36.3 0.0 copy-start.1
  36.3 0.2 fusion.20
  36.5 0.4 fusion.2
  36.9 0.0 copy-start.2
  36.9 0.1 fusion.27
  37.0 0.4 collective-permute-start.2
  37.4 0.0 collective-permute-done.1
  37.5 2.3 %collective-permute-start.3 = (bf16[64,1,128]{2,0,1:T(8,128)(2,1)S(1)}, bf16[64,1,128]{2,0,1:T(8,128)(2,1)}, u32[]{:S(2)}, u32[]{:S(2)}) collective-permute-start(bf16[64,1,128]{2,0,1:T(8,128)(2,1)S(1)} %collective-permute-done.1), channel_id=1, source_target_pairs={{0,28},{4,0},{8,4},{12,8},{16,12},{20,16},{24,20},{28,24},{1,29},{... | collective-permute-start | bytes 49160 | tf_op jit(solution)/shard_map/ppermute | solution.py:16
  39.8 1.3 %collective-permute-done.2 = bf16[64,1,128]{2,0,1:T(8,128)(2,1)S(1)} collective-permute-done((bf16[64,1,128]{2,0,1:T(8,128)(2,1)S(1)}, bf16[64,1,128]{2,0,1:T(8,128)(2,1)S(1)}, u32[]{:S(2)}, u32[]{:S(2)}) %collective-permute-start.2) | collective-permute-done | bytes 16416 | tf_op jit(solution)/shard_map/ppermute | solution.py:13
  41.2 0.3 fusion.9
  41.4 9.3 %all_gather.11 = bf16[256,1,128]{2,0,1:T(8,128)(2,1)S(1)} all-gather(bf16[32,1,128]{2,0,1:T(8,128)(2,1)S(1)} %get-tuple-element.15), channel_id=1, replica_groups=mesh['ctx'=8,'tp'=4] {'ctx'}, dimensions={0}, use_global_device_ids=true | all-gather | bytes 73728 | tf_op jit(solution)/shard_map/all_gather | solution.py:95
  50.7 1.5 %collective-permute-start.5 = (bf16[64,1,128]{2,0,1:T(8,128)(2,1)}, bf16[64,1,128]{2,0,1:T(8,128)(2,1)}, u32[]{:S(2)}, u32[]{:S(2)}) collective-permute-start(bf16[64,1,128]{2,0,1:T(8,128)(2,1)} %collective-permute-done.3), channel_id=1, source_target_pairs={{0,28},{4,0},{8,4},{12,8},{16,12},{20,16},{24,20},{28,24},{1,29},{... | collective-permute-start | bytes 49160 | tf_op jit(solution)/shard_map/ppermute | solution.py:16
  52.2 0.3 convolution_bitcast_fusion
  52.7 0.7 copy.47
  53.4 0.9 dynamic_update_slice.32
  54.4 1.4 %copy.48 = bf16[64,128]{0,1:T(8,128)(2,1)} copy(bf16[64,128]{1,0:T(8,128)(2,1)} %bitcast.118) | data formatting | bytes 32768 | tf_op jit(solution)/shard_map/reshape.150
  55.8 1.4 %copy.49 = bf16[64,128]{0,1:T(8,128)(2,1)} copy(bf16[64,128]{1,0:T(8,128)(2,1)} %bitcast.119) | data formatting | bytes 32768 | tf_op jit(solution)/shard_map/reshape.148
  57.2 1.1 dynamic_update_slice.33
  58.3 1.1 dynamic_update_slice.34
  59.4 1.4 %copy.50 = bf16[64,128]{0,1:T(8,128)(2,1)} copy(bf16[64,128]{1,0:T(8,128)(2,1)} %bitcast.120) | data formatting | bytes 32768 | tf_op jit(solution)/shard_map/reshape.146
  60.9 1.4 %copy.51 = bf16[64,128]{0,1:T(8,128)(2,1)} copy(bf16[64,128]{1,0:T(8,128)(2,1)} %bitcast.17) | data formatting | bytes 32768 | tf_op jit(solution)/shard_map/reshape.144
  62.3 0.9 dynamic_update_slice.35
  63.2 0.9 dynamic_update_slice.36
  64.1 1.4 %copy.52 = bf16[64,128]{0,1:T(8,128)(2,1)} copy(bf16[64,128]{1,0:T(8,128)(2,1)} %bitcast.18) | data formatting | bytes 32768 | tf_op jit(solution)/shard_map/reshape.142
  65.6 1.4 %copy.53 = bf16[64,128]{0,1:T(8,128)(2,1)} copy(bf16[64,128]{1,0:T(8,128)(2,1)} %bitcast.19) | data formatting | bytes 32768 | tf_op jit(solution)/shard_map/reshape.140
  67.0 1.1 dynamic_update_slice.37
  68.1 1.1 dynamic_update_slice.38
  69.2 1.4 %copy.54 = bf16[64,128]{0,1:T(8,128)(2,1)} copy(bf16[64,128]{1,0:T(8,128)(2,1)} %bitcast.20) | data formatting | bytes 32768 | tf_op jit(solution)/shard_map/reshape.115
  70.7 0.9 dynamic_update_slice.39
  71.6 0.5 fusion.14
  72.1 7.3 %fusion = bf16[4096,128]{0,1:T(8,128)(2,1)} fusion(bf16[128,1024]{0,1:T(8,128)(2,1)S(1)} %bitcast.116, bf16[4096,1024]{1,0:T(8,128)(2,1)} %param.17), kind=kOutput, calls=%fused_computation.3 | convolution fusion | flops 1074266112 | bytes 9699328 | tf_op jit(solution)/shard_map/dot_general | solution.py:108
  79.4 0.0 reduce-scatter.2.cloned.1.call-update
  79.4 28.9 %reduce-scatter.2.cloned.1.call-done = bf16[1024,128]{0,1:T(8,128)(2,1)} async-done(((bf16[4096,128]{0,1:T(8,128)(2,1)}), bf16[1024,128]{0,1:T(8,128)(2,1)}) %reduce-scatter.2.cloned.1.call-update) | async-done | bytes 262160 | tf_op jit(solution)/shard_map/reduce_scatter | solution.py:107
  108.3 1.8 %copy.59 = bf16[1024,128]{1,0:T(8,128)(2,1)} copy(bf16[1024,128]{0,1:T(8,128)(2,1)} %reduce-scatter.2.cloned.1.call-done) | data formatting | bytes 524288 | tf_op jit(solution)/shard_map/reduce_scatter | solution.py:107
  (24 shorter events, 0.1 us)
Async XLA Ops:
  6.5 27.3 %copy-start = (bf16[128,8,128]{2,1,0:T(8,128)(2,1)S(1)}, bf16[128,8,128]{2,1,0:T(8,128)(2,1)}, u32[]{:S(2)}) copy-start(bf16[128,8,128]{2,1,0:T(8,128)(2,1)} %param.10) | copy-start | bytes 786436
  6.5 101.8 %reduce-scatter.2.cloned.1.call-start = ((), (), s32[]{:S(2)}) async-start(), calls=%async_computation.1 | async-start | bytes 1310720 | tf_op jit(solution)/shard_map/reduce_scatter | solution.py:107
  6.5 30.5 %collective-permute-start = (bf16[64,1,128]{2,0,1:T(8,128)(2,1)}, bf16[64,1,128]{2,0,1:T(8,128)(2,1)S(1)}, u32[]{:S(2)}, u32[]{:S(2)}) collective-permute-start(bf16[64,1,128]{2,0,1:T(8,128)(2,1)} %param.14), channel_id=1, source_target_pairs={{0,4},{4,8},{8,12},{12,16},{16,20},{20,24},{24,28},{28,0},{1,5},{5... | collective-permute-start | bytes 49160 | tf_op jit(solution)/shard_map/ppermute | solution.py:13
  7.0 30.4 %collective-permute-start.1 = (bf16[64,1,128]{2,0,1:T(8,128)(2,1)}, bf16[64,1,128]{2,0,1:T(8,128)(2,1)S(1)}, u32[]{:S(2)}, u32[]{:S(2)}) collective-permute-start(bf16[64,1,128]{2,0,1:T(8,128)(2,1)} %param.14), channel_id=1, source_target_pairs={{0,28},{4,0},{8,4},{12,8},{16,12},{20,16},{24,20},{28,24},{1,29},{... | collective-permute-start | bytes 49160 | tf_op jit(solution)/shard_map/ppermute | solution.py:16
  36.3 4.9 %copy-start.1 = (bf16[128,1,128]{2,0,1:T(8,128)(2,1)S(1)}, bf16[128,1,128]{2,0,1:T(8,128)(2,1)}, u32[]{:S(2)}) copy-start(bf16[128,1,128]{2,0,1:T(8,128)(2,1)} %param.12) | copy-start | bytes 98308
  36.9 15.8 %copy-start.2 = (bf16[64,1,128]{2,0,1:T(8,128)(2,1)S(1)}, bf16[64,1,128]{2,0,1:T(8,128)(2,1)}, u32[]{:S(2)}) copy-start(bf16[64,1,128]{2,0,1:T(8,128)(2,1)} %param.14) | copy-start | bytes 49156
  37.0 16.4 %copy-start.3 = (bf16[64,1,128]{2,0,1:T(8,128)(2,1)}, bf16[64,1,128]{2,0,1:T(8,128)(2,1)S(1)}, u32[]{:S(2)}) copy-start(bf16[64,1,128]{2,0,1:T(8,128)(2,1)S(1)} %collective-permute-done) | copy-start | bytes 49156
  37.0 4.1 %collective-permute-start.2 = (bf16[64,1,128]{2,0,1:T(8,128)(2,1)S(1)}, bf16[64,1,128]{2,0,1:T(8,128)(2,1)S(1)}, u32[]{:S(2)}, u32[]{:S(2)}) collective-permute-start(bf16[64,1,128]{2,0,1:T(8,128)(2,1)S(1)} %collective-permute-done), channel_id=1, source_target_pairs={{0,4},{4,8},{8,12},{12,16},{16,20},{20,24},{24,28},{28,0},{1,5},{5... | collective-permute-start | bytes 49160 | tf_op jit(solution)/shard_map/ppermute | solution.py:13
  37.5 16.0 %copy-start.4 = (bf16[64,1,128]{2,0,1:T(8,128)(2,1)}, bf16[64,1,128]{2,0,1:T(8,128)(2,1)S(1)}, u32[]{:S(2)}) copy-start(bf16[64,1,128]{2,0,1:T(8,128)(2,1)S(1)} %collective-permute-done.1) | copy-start | bytes 49156
  37.5 13.3 %collective-permute-start.3 = (bf16[64,1,128]{2,0,1:T(8,128)(2,1)S(1)}, bf16[64,1,128]{2,0,1:T(8,128)(2,1)}, u32[]{:S(2)}, u32[]{:S(2)}) collective-permute-start(bf16[64,1,128]{2,0,1:T(8,128)(2,1)S(1)} %collective-permute-done.1), channel_id=1, source_target_pairs={{0,28},{4,0},{8,4},{12,8},{16,12},{20,16},{24,20},{28,24},{1,29},{... | collective-permute-start | bytes 49160 | tf_op jit(solution)/shard_map/ppermute | solution.py:16
  41.1 12.3 %copy-start.5 = (bf16[64,1,128]{2,0,1:T(8,128)(2,1)}, bf16[64,1,128]{2,0,1:T(8,128)(2,1)S(1)}, u32[]{:S(2)}) copy-start(bf16[64,1,128]{2,0,1:T(8,128)(2,1)S(1)} %collective-permute-done.2) | copy-start | bytes 49156
  41.1 11.0 %collective-permute-start.4 = (bf16[64,1,128]{2,0,1:T(8,128)(2,1)S(1)}, bf16[64,1,128]{2,0,1:T(8,128)(2,1)}, u32[]{:S(2)}, u32[]{:S(2)}) collective-permute-start(bf16[64,1,128]{2,0,1:T(8,128)(2,1)S(1)} %collective-permute-done.2), channel_id=1, source_target_pairs={{0,4},{4,8},{8,12},{12,16},{16,20},{20,24},{24,28},{28,0},{1,5},{5... | collective-permute-start | bytes 49160 | tf_op jit(solution)/shard_map/ppermute | solution.py:13
  50.7 14.8 %collective-permute-start.5 = (bf16[64,1,128]{2,0,1:T(8,128)(2,1)}, bf16[64,1,128]{2,0,1:T(8,128)(2,1)}, u32[]{:S(2)}, u32[]{:S(2)}) collective-permute-start(bf16[64,1,128]{2,0,1:T(8,128)(2,1)} %collective-permute-done.3), channel_id=1, source_target_pairs={{0,28},{4,0},{8,4},{12,8},{16,12},{20,16},{24,20},{28,24},{1,29},{... | collective-permute-start | bytes 49160 | tf_op jit(solution)/shard_map/ppermute | solution.py:16
  52.2 17.0 %collective-permute-start.6 = (bf16[64,1,128]{2,0,1:T(8,128)(2,1)}, bf16[64,1,128]{2,0,1:T(8,128)(2,1)}, u32[]{:S(2)}, u32[]{:S(2)}) collective-permute-start(bf16[64,1,128]{2,0,1:T(8,128)(2,1)} %collective-permute-done.4), channel_id=1, source_target_pairs={{0,4},{4,8},{8,12},{12,16},{16,20},{20,24},{24,28},{28,0},{1,5},{5... | collective-permute-start | bytes 49160 | tf_op jit(solution)/shard_map/ppermute | solution.py:13
Sparse Core Ops, SparseCore 0:
  79.5 28.7 reduce-scatter.1
